TPU v7x, 32 devices: a whole 2x2x4 slice. The times are simulated.
32 devices in a mesh: ctx: 8 (over z, x), head: 4 (over y, core).
Axes of the slice: x: 2, y: 2, z: 4, core: 2. Of those that a mesh axis runs over, the one named last changes fastest.
Arguments:
- token_keys: bfloat16 [8, 2048, 128], P(None, ('ctx', 'head')), may hold values from -4.5 to 4.5
- token_values: bfloat16 [8, 2048, 128], P(None, ('ctx', 'head')), may hold values from -6 to 6
- queries: bfloat16 [8, 2048, 8, 128], P(None, ('ctx', 'head')), may hold values from -16 to 16
- out_grad: bfloat16 [8, 2048, 8, 128], P(None, ('ctx', 'head')), may hold values from -6 to 6
- slot_ids: int32 [8, 2048], P('head'), may hold values from 0 to 511, as said below
Outputs:
- attended: bfloat16 [8, 2048, 8, 128], P(None, ('ctx', 'head'))
- key_grad: float32 [8, 2048, 128], P(None, ('ctx', 'head'))
- value_grad: float32 [8, 2048, 128], P(None, ('ctx', 'head'))
Inputs may be any that keep to these rules, and one draw needn't show every extreme that they name: `slot_ids`: in each head's row slot numbers never fall; each of the 512 slots holds 1 to 16 consecutive tokens; slots k * 64 to (k + 1) * 64 - 1 all begin among tokens k * 256 to (k + 1) * 256 - 1; every such block of tokens holds a slot of exactly 16 tokens.
All inputs are finite; a program needn't handle non-finite values.
Results may differ from a plain program's by a relative error of at most 0.012.
The roundings to bfloat16 on the way count: a program that leaves them out, or rounds other values in their place, can miss the bound.
Values may be sent and summed in bfloat16 or wider, within the bound.
A program may use at most 64 MiB of HBM per device.

v0:
```python
import math
import jax
import jax.numpy as jnp
from jax import lax
from jax.sharding import PartitionSpec as P

RATIO = 4
neg_big = -1e30


def from_behind(value, axis, steps):
    count = lax.axis_size(axis)
    initial, last = (max(0, -steps), min(count, count - steps))
    return lax.ppermute(value, axis, [(source, source + steps) for source in range(initial, last)])


def one_hot_rows(own_ids, first_row, how_many):
    relative = own_ids - first_row
    columns = jnp.arange(how_many, dtype=jnp.int32)
    return (relative[:, :, None] == columns[None, None, :]).astype(jnp.bfloat16)


def per_device(token_keys, token_values, queries, out_grad, slot_ids):
    keys_here, values_here, query_here, grad_here = (
        lax.all_to_all(token_keys, "head", split_axis=0, concat_axis=1, tiled=True),
        lax.all_to_all(token_values, "head", split_axis=0, concat_axis=1, tiled=True),
        lax.all_to_all(queries, "head", split_axis=0, concat_axis=1, tiled=True),
        lax.all_to_all(out_grad, "head", split_axis=0, concat_axis=1, tiled=True),
    )
    local_heads, tok_count, head_dim = keys_here.shape
    query_count = query_here.shape[1]
    group_size = query_here.shape[2]
    slot_count = tok_count // RATIO
    id_heads, context_len = slot_ids.shape
    total_slots = context_len // RATIO
    block_count = context_len // tok_count
    ctx_index = lax.axis_index("ctx")
    blocked_ids = slot_ids.reshape(id_heads, block_count, tok_count)
    block_base = jnp.arange(block_count, dtype=jnp.int32)
    targets = block_base[:, None] * slot_count + jnp.arange(slot_count, dtype=jnp.int32)[None, :]
    below_count = jnp.sum(
        (blocked_ids[:, :, :, None] < targets[None, :, None, :]).astype(jnp.int32), axis=2
    )
    starts_all = (block_base[None, :, None] * tok_count + below_count).reshape(
        id_heads, total_slots
    )
    slot_edges = jnp.concatenate(
        [starts_all, jnp.full((id_heads, 1), context_len, jnp.int32)], axis=1
    )
    slot_start = starts_all.T
    slot_len = slot_edges[:, 1:] - slot_edges[:, :-1]
    lengths_t = slot_len.T.astype(jnp.float32)[:, :, None]
    own_ids = lax.dynamic_slice_in_dim(slot_ids, ctx_index * tok_count, tok_count, 1)
    pair_low = jnp.concatenate([keys_here, values_here], axis=2)
    first_slot = ctx_index * slot_count - 1
    hot = one_hot_rows(own_ids, first_slot, slot_count + 1)
    window = jnp.einsum("htn,htc->nhc", hot, pair_low, preferred_element_type=jnp.float32)
    carried = from_behind(window[:1], "ctx", -1)
    padding = jnp.zeros((slot_count - 1, local_heads, 2 * head_dim), jnp.float32)
    own_sums = window[1:] + jnp.concatenate([padding, carried], axis=0)
    own_len = lax.dynamic_slice_in_dim(lengths_t, ctx_index * slot_count, slot_count, 0)
    slot_pairs = (own_sums / own_len).astype(jnp.bfloat16)
    rows_here = query_count * group_size
    query_rows = query_here.reshape(local_heads, rows_here, head_dim)
    grad_rows = grad_here.reshape(local_heads, rows_here, head_dim)
    stride = tok_count // query_count
    positions = jnp.repeat(
        (ctx_index * query_count + jnp.arange(query_count, dtype=jnp.int32)) * stride + stride - 1,
        group_size,
    )
    last_position = (ctx_index + 1) * query_count * stride - 1
    score_scale = 1.0 / math.sqrt(head_dim)

    def block_scores(key_block):
        scores = (
            jnp.einsum("hrd,nhd->hrn", query_rows, key_block, preferred_element_type=jnp.float32)
            * score_scale
        )
        visible = slot_start.T[:, None, :] <= positions[None, :, None]
        return (scores, visible)

    def reaches(first_row):
        return (
            jnp.min(lax.dynamic_index_in_dim(slot_start, first_row, 0, keepdims=False))
            <= last_position
        )

    init_stats = (
        jnp.full((local_heads, rows_here), neg_big, jnp.float32),
        jnp.zeros((local_heads, rows_here), jnp.float32),
    )
    key_block = lax.all_gather(slot_pairs[:, :, :head_dim], "ctx", axis=0, tiled=True)

    def stats_advance(state_in):
        top_now, mass_now = state_in
        scores, visible = block_scores(key_block)
        top_new = jnp.maximum(top_now, jnp.max(jnp.where(visible, scores, neg_big), axis=2))
        fresh = jnp.sum(jnp.where(visible, jnp.exp(scores - top_new[:, :, None]), 0.0), axis=2)
        return (top_new, fresh)

    row_top, row_mass = lax.cond(
        reaches(jnp.int32(0)), stats_advance, lambda state_in: state_in, init_stats
    )
    log_total = row_top + jnp.log(row_mass)

    def weights_of(pair_block):
        scores, visible = block_scores(pair_block[:, :, :head_dim])
        return jnp.where(visible, jnp.exp(scores - log_total[:, :, None]), 0.0)

    init_acc = jnp.zeros((local_heads, rows_here, head_dim), jnp.float32)
    pair_block = lax.all_gather(slot_pairs, "ctx", axis=0, tiled=True)

    def value_advance(state_in):
        weights_low = weights_of(pair_block).astype(jnp.bfloat16)
        return jnp.einsum(
            "hrn,nhd->hrd",
            weights_low,
            pair_block[:, :, head_dim:],
            preferred_element_type=jnp.float32,
        )

    summed_out = lax.cond(reaches(jnp.int32(0)), value_advance, lambda state_in: state_in, init_acc)
    attended = summed_out.astype(jnp.bfloat16)
    out_back = lax.all_to_all(
        attended.reshape(local_heads, query_count, group_size, head_dim),
        "head",
        split_axis=1,
        concat_axis=0,
        tiled=True,
    )
    row_dot = jnp.sum(grad_rows.astype(jnp.float32) * attended.astype(jnp.float32), axis=2)
    init_partials = jnp.zeros((total_slots, local_heads, 2 * head_dim), jnp.float32)
    grad_pair_block = lax.all_gather(slot_pairs, "ctx", axis=0, tiled=True)

    def grad_advance(state_in):
        weights = weights_of(grad_pair_block)
        weights_low = weights.astype(jnp.bfloat16)
        value_grads = jnp.einsum(
            "hrn,hrd->nhd", weights_low, grad_rows, preferred_element_type=jnp.float32
        )
        weight_grads = jnp.einsum(
            "hrd,nhd->hrn",
            grad_rows,
            grad_pair_block[:, :, head_dim:],
            preferred_element_type=jnp.float32,
        )
        dscores = (weights * (weight_grads - row_dot[:, :, None])).astype(jnp.bfloat16)
        key_grads = (
            jnp.einsum("hrn,hrd->nhd", dscores, query_rows, preferred_element_type=jnp.float32)
            * score_scale
        )
        return jnp.concatenate([key_grads, value_grads], axis=2)

    partials = lax.cond(
        reaches(jnp.int32(0)), grad_advance, lambda state_in: state_in, init_partials
    )
    share_grads = lax.psum_scatter(
        partials.astype(jnp.bfloat16), "ctx", scatter_dimension=0, tiled=True
    )
    below_row = from_behind(share_grads[-1:], "ctx", 1)
    grad_window = jnp.concatenate([below_row, share_grads], axis=0)
    hot = one_hot_rows(own_ids, first_slot, grad_window.shape[0])
    token_sums = jnp.einsum("htn,nhc->htc", hot, grad_window, preferred_element_type=jnp.float32)
    padded_len = jnp.concatenate([jnp.ones((id_heads, 1), jnp.int32), slot_len], axis=1)
    window_len = lax.dynamic_slice_in_dim(padded_len, first_slot + 1, slot_count + 1, 1).astype(
        jnp.float32
    )
    relative_ids = own_ids - first_slot
    window_cols = jnp.arange(slot_count + 1, dtype=jnp.int32)
    token_len = jnp.sum(
        jnp.where(
            relative_ids[:, :, None] == window_cols[None, None, :], window_len[:, None, :], 0.0
        ),
        axis=2,
    )[:, :, None]
    token_grads = token_sums / token_len
    key_back, value_back = (
        lax.all_to_all(
            token_grads[:, :, :head_dim].astype(jnp.bfloat16),
            "head",
            split_axis=1,
            concat_axis=0,
            tiled=True,
        ).astype(jnp.float32),
        lax.all_to_all(
            token_grads[:, :, head_dim:].astype(jnp.bfloat16),
            "head",
            split_axis=1,
            concat_axis=0,
            tiled=True,
        ).astype(jnp.float32),
    )
    return (out_back, key_back, value_back)


def solution(mesh):
    placed = (
        P(None, ("ctx", "head"), None),
        P(None, ("ctx", "head"), None),
        P(None, ("ctx", "head"), None, None),
        P(None, ("ctx", "head"), None, None),
        P("head", None),
    )
    return jax.shard_map(
        per_device,
        mesh=mesh,
        in_specs=placed,
        out_specs=(
            P(None, ("ctx", "head"), None, None),
            P(None, ("ctx", "head"), None),
            P(None, ("ctx", "head"), None),
        ),
        check_vma=False,
    )
```

profile of v0, /device:TPU:8, one launch (start us, length us, event | category | flops | bytes accessed | tf_op | source)
XLA Modules:
  0.0 240.5 jit_solution(12412605172236448797)
XLA Ops:
  7.2 3.3 %all-to-all-start = ((bf16[8,64,128]{2,1,0:T(8,128)(2,1)}), bf16[8,64,128]{2,1,0:T(8,128)(2,1)S(1)}, u32[]{:S(2)}, u32[]{:S(2)}) async-start(bf16[8,64,128]{2,1,0:T(8,128)(2,1)} %param.11), calls=%async_computation | async-start | bytes 262144 | tf_op jit(solution)/shard_map/all_to_all | solution.py:25
  10.6 0.7 copy.73
  11.3 0.5 convert_reduce_fusion
  11.8 0.7 dynamic-slice_subtract_fusion
  12.5 2.6 %all-to-all-done = bf16[8,64,128]{2,1,0:T(8,128)(2,1)S(1)} async-done(((bf16[8,64,128]{2,1,0:T(8,128)(2,1)}), bf16[8,64,128]{2,1,0:T(8,128)(2,1)S(1)}, u32[]{:S(2)}, u32[]{:S(2)}) %all-to-all-start) | async-done | bytes 131104 | tf_op jit(solution)/shard_map/all_to_all | solution.py:25
  15.1 3.3 %all-to-all-start.1 = ((bf16[8,64,128]{2,1,0:T(8,128)(2,1)}), bf16[8,64,128]{2,1,0:T(8,128)(2,1)S(1)}, u32[]{:S(2)}, u32[]{:S(2)}) async-start(bf16[8,64,128]{2,1,0:T(8,128)(2,1)} %param.12), calls=%async_computation.1 | async-start | bytes 262144 | tf_op jit(solution)/shard_map/all_to_all | solution.py:26
  18.5 4.6 %all-to-all-done.1 = bf16[8,64,128]{2,1,0:T(8,128)(2,1)S(1)} async-done(((bf16[8,64,128]{2,1,0:T(8,128)(2,1)}), bf16[8,64,128]{2,1,0:T(8,128)(2,1)S(1)}, u32[]{:S(2)}, u32[]{:S(2)}) %all-to-all-start.1) | async-done | bytes 131104 | tf_op jit(solution)/shard_map/all_to_all | solution.py:26
  23.0 3.5 %all-to-all-start.2 = ((bf16[8,64,8,128]{3,2,1,0:T(8,128)(2,1)}), bf16[8,64,8,128]{3,2,1,0:T(8,128)(2,1)S(1)}, u32[]{:S(2)}, u32[]{:S(2)}) async-start(bf16[8,64,8,128]{3,2,1,0:T(8,128)(2,1)} %param.13), calls=%async_computation.2 | async-start | bytes 2097152 | tf_op jit(solution)/shard_map/all_to_all | solution.py:27
  26.8 0.6 slice_reduce_fusion
  27.6 13.4 %all-to-all-done.2 = bf16[8,64,8,128]{3,2,1,0:T(8,128)(2,1)S(1)} async-done(((bf16[8,64,8,128]{3,2,1,0:T(8,128)(2,1)}), bf16[8,64,8,128]{3,2,1,0:T(8,128)(2,1)S(1)}, u32[]{:S(2)}, u32[]{:S(2)}) %all-to-all-start.2) | async-done | bytes 1048608 | tf_op jit(solution)/shard_map/all_to_all | solution.py:27
  41.0 4.3 %all-to-all-start.4 = ((bf16[8,64,8,128]{3,2,1,0:T(8,128)(2,1)}), bf16[8,64,8,128]{3,2,1,0:T(8,128)(2,1)}, u32[]{:S(2)}, u32[]{:S(2)}) async-start(bf16[8,64,8,128]{3,2,1,0:T(8,128)(2,1)} %param.14), calls=%async_computation.4 | async-start | bytes 2097152 | tf_op jit(solution)/shard_map/all_to_all | solution.py:28
  45.3 0.2 convolution_bitcast_fusion
  45.5 3.3 %collective-permute-start = (f32[1,2,256]{2,0,1:T(1,128)S(1)}, f32[1,2,256]{2,0,1:T(1,128)S(1)}, u32[]{:S(2)}, u32[]{:S(2)}) collective-permute-start(f32[1,2,256]{2,0,1:T(1,128)S(1)} %slice.50), channel_id=1, source_target_pairs={{4,0},{8,4},{12,8},{16,12},{20,16},{24,20},{28,24},{5,1},{9,5},{13... | collective-permute-start | bytes 6152 | tf_op jit(solution)/shard_map/ppermute | solution.py:14
  49.5 1.5 collective-permute-done
  51.1 28.4 %all_gather.8 = bf16[512,2,128]{2,0,1:T(8,128)(2,1)S(1)} all-gather(bf16[64,2,128]{2,0,1:T(8,128)(2,1)S(1)} %slice.51), channel_id=1, replica_groups=mesh['ctx'=8,'head'=4] {'ctx'}, dimensions={0}, use_global_device_ids=true | all-gather | bytes 294912 | tf_op jit(solution)/shard_map/all_gather | solution.py:92
  79.5 31.5 %all_gather.7 = bf16[512,2,256]{2,0,1:T(8,128)(2,1)S(1)} all-gather(bf16[64,2,256]{2,0,1:T(8,128)(2,1)S(1)} %fusion.31), channel_id=1, replica_groups=mesh['ctx'=8,'head'=4] {'ctx'}, dimensions={0}, use_global_device_ids=true | all-gather | bytes 589824 | tf_op jit(solution)/shard_map/all_gather | solution.py:111
  111.1 4.9 %conditional.3 = (f32[2,2048]{1,0:T(2,128)}, f32[2,2048]{1,0:T(2,128)S(1)}) conditional(s32[]{:T(128)} %convert_element_type.72, () %tuple.34, (s32[2,8,64]{2,1,0:T(8,128)S(1)}, s32[256,8]{1,0:T(8,128)S(1)}, bf16[2,2048,128]{2,1,0:T(8,128)(2,1)S(1)}, bf16[512,2,128]{2,0,1:T(8,128)(2,1)S(1)}) %tuple.56), branch_computations={%region_2.3_spmd, %region_3.6_spmd} | conditional | flops 555741184 | bytes 18251792 | solution.py:101
  111.3 1.3 fusion
  112.7 0.6 broadcast_maximum_fusion
  113.3 2.7 %fusion.1 = f32[2,2048]{1,0:T(2,128)S(1)} fusion(f32[2,2048,512]{1,2,0:T(8,128)S(1)} %get-tuple-element.122, f32[2,2048]{1,0:T(2,128)} %broadcast_maximum_fusion, s32[2048]{0:T(1024)S(1)} %le.37, s32[2,512]{1,0:T(2,128)S(1)} %le.35), kind=kLoop, calls=%fused_computation.3 | loop fusion | flops 10481664 | bytes 8433664 | tf_op jit(solution)/shard_map/cond/branch_1_fun/reduce_sum | solution.py:98
  116.1 1.3 add.98
  117.4 3.5 %conditional.4 = (bf16[2,2048,128]{2,1,0:T(8,128)(2,1)S(1)}) conditional(s32[]{:T(128)} %convert_element_type.72, () %tuple.33, (s32[2,8,64]{2,1,0:T(8,128)S(1)}, s32[256,8]{1,0:T(8,128)S(1)}, bf16[512,2,256]{2,0,1:T(8,128)(2,1)S(1)}, bf16[2,2048,128]{2,1,0:T(8,128)(2,1)S(1)}, f32[2,2048]{1,0:T(2,128)}) %tuple.57), branch_computations={%region_6.7_spmd, %region_7.8_spmd} | conditional | flops 1084227584 | bytes 2674696 | solution.py:122
  117.6 3.3 %fusion.2 = bf16[2,2048,128]{2,1,0:T(8,128)(2,1)S(1)} fusion(bf16[2,2048,128]{2,1,0:T(8,128)(2,1)S(1)} %get-tuple-element.67, f32[2,2048]{1,0:T(2,128)} %get-tuple-element.69, s32[2,512]{1,0:T(2,128)S(1)} %le.50, s32[2048]{0:T(1024)S(1)} %le.52, bf16[512,2,256]{2,0,1:T(8,128)(2,1)S(1)} %get-tuple-element.68), kind=kOutput, calls=%fused_computation.6 | convolution fusion | flops 1084227584 | bytes 2650112 | tf_op jit(solution)/shard_map/cond/branch_1_fun/hrn,nhd->hrd/dot_general | solution.py:115
  121.1 21.8 %conditional.5 = (bf16[512,2,256]{0,2,1:T(8,128)(2,1)S(1)}) conditional(s32[]{:T(128)} %convert_element_type.72, () %tuple.37, (s32[2,8,64]{2,1,0:T(8,128)S(1)}, s32[256,8]{1,0:T(8,128)S(1)}, bf16[512,2,256]{2,0,1:T(8,128)(2,1)}, bf16[2,2048,128]{2,1,0:T(8,128)(2,1)}, f32[2,2048]{1,0:T(2,128)}, /*index=5*/bf16[2,4,64,8,128]{4,3,2,0,1:T(8,128)(2,1)}, ...), branch_computations={%region_8.9_spmd, %region_9.11_spmd} | conditional | flops 2175528960 | bytes 49414264 | solution.py:154
  121.3 0.7 le.55
  122.1 1.3 copy.62
  123.4 0.7 multiply_reduce_fusion
  124.1 0.3 copy-done.2
  124.4 5.9 %fusion.20 = f32[2,2048,512]{2,1,0:T(8,128)} fusion(bf16[2,2048,128]{2,1,0:T(8,128)(2,1)} %get-tuple-element.117, bf16[512,2,256]{2,0,1:T(8,128)(2,1)} %get-tuple-element.73), kind=kOutput, calls=%fused_computation.23 | convolution fusion | flops 536870912 | bytes 9699328 | tf_op jit(solution)/shard_map/cond/branch_1_fun/hrd,nhd->hrn/dot_general | solution.py:76
  130.3 7.0 %fusion.17 = bf16[512,2,128]{0,2,1:T(8,128)(2,1)S(1)} fusion(bf16[2,2048,128]{2,1,0:T(8,128)(2,1)S(1)} %copy-done.1, f32[2,2048,512]{2,1,0:T(8,128)} %fusion.20, bf16[2,2048,128]{2,1,0:T(8,128)(2,1)S(1)} %bitcast.57, f32[2,2048]{1,0:T(2,128)S(1)} %multiply_reduce_fusion, f32[2,2048]{1,0:T(2,128)} %get-tuple-element.74, s32[2,512]{1,0:T(2,128)S(1)} %copy-done.5, ...), kind=kOutput, calls=%fused_computation.20 | convolution fusion | flops 1088684032 | bytes 11055104 | tf_op jit(solution)/shard_map/cond/branch_1_fun/hrn,hrd->nhd/dot_general | solution.py:149
  137.2 5.6 %fusion.13 = bf16[512,2,128]{0,2,1:T(8,128)(2,1)S(1)} fusion(bf16[2,2048,128]{2,1,0:T(8,128)(2,1)S(1)} %bitcast.58, f32[2,2048,512]{2,1,0:T(8,128)} %fusion.20, f32[2,2048]{1,0:T(2,128)} %get-tuple-element.74, s32[2,512]{1,0:T(2,128)S(1)} %copy-done.5, s32[2048]{0:T(1024)S(1)} %le.57), kind=kOutput, calls=%fused_computation.18 | convolution fusion | flops 547356672 | bytes 9728000 | tf_op jit(solution)/shard_map/cond/branch_1_fun/hrn,hrd->nhd/dot_general | solution.py:138
  142.9 1.0 copy.63
  144.0 1.2 copy.58
  145.1 3.5 %all-to-all-start.3 = ((bf16[2,256,8,128]{3,2,0,1:T(8,128)(2,1)}), bf16[2,256,8,128]{3,2,0,1:T(8,128)(2,1)S(1)}, u32[]{:S(2)}, u32[]{:S(2)}) async-start(bf16[2,256,8,128]{3,2,0,1:T(8,128)(2,1)} %copy.58), calls=%async_computation.3 | async-start | bytes 2097152 | tf_op jit(solution)/shard_map/all_to_all | solution.py:124
  148.7 59.2 %reduce-scatter.2.cloned.1.call-done = bf16[64,2,256]{2,0,1:T(8,128)(2,1)} async-done(((bf16[512,2,256]{2,0,1:T(8,128)(2,1)}), bf16[64,2,256]{2,0,1:T(8,128)(2,1)}) %reduce-scatter.2.cloned.1.call-update) | async-done | bytes 65552 | tf_op jit(solution)/shard_map/reduce_scatter | solution.py:157
  207.9 0.7 slice.52
  208.6 3.4 %collective-permute-start.1 = (bf16[1,2,256]{2,0,1:T(2,128)(2,1)S(1)}, bf16[1,2,256]{2,0,1:T(2,128)(2,1)S(1)}, u32[]{:S(2)}, u32[]{:S(2)}) collective-permute-start(bf16[1,2,256]{2,0,1:T(2,128)(2,1)S(1)} %slice.52), channel_id=1, source_target_pairs={{0,4},{4,8},{8,12},{12,16},{16,20},{20,24},{24,28},{1,5},{5,9},{9,... | collective-permute-start | bytes 3080 | tf_op jit(solution)/shard_map/ppermute | solution.py:14
  212.1 2.9 %collective-permute-done.1 = bf16[1,2,256]{2,0,1:T(2,128)(2,1)S(1)} collective-permute-done((bf16[1,2,256]{2,0,1:T(2,128)(2,1)S(1)}, bf16[1,2,256]{2,0,1:T(2,128)(2,1)S(1)}, u32[]{:S(2)}, u32[]{:S(2)}) %collective-permute-start.1) | collective-permute-done | bytes 1056 | tf_op jit(solution)/shard_map/ppermute | solution.py:14
  215.0 1.1 fusion.26
  216.2 0.8 copy.66
  217.0 3.3 %all-to-all-start.6 = ((bf16[2,256,128]{2,0,1:T(2,128)(2,1)}), bf16[2,256,128]{2,0,1:T(2,128)(2,1)S(1)}, u32[]{:S(2)}, u32[]{:S(2)}) async-start(bf16[2,256,128]{2,0,1:T(2,128)(2,1)} %copy.66), calls=%async_computation.7 | async-start | bytes 262144 | tf_op jit(solution)/shard_map/all_to_all | solution.py:185
  220.3 1.2 copy.60
  221.5 0.8 copy.64
  222.3 2.6 %all-to-all-done.6 = bf16[2,256,128]{2,0,1:T(2,128)(2,1)S(1)} async-done(((bf16[2,256,128]{2,0,1:T(2,128)(2,1)}), bf16[2,256,128]{2,0,1:T(2,128)(2,1)S(1)}, u32[]{:S(2)}, u32[]{:S(2)}) %all-to-all-start.6) | async-done | bytes 131104 | tf_op jit(solution)/shard_map/all_to_all | solution.py:185
  224.9 3.3 %all-to-all-start.5 = ((bf16[2,256,128]{2,0,1:T(2,128)(2,1)}), bf16[2,256,128]{2,0,1:T(2,128)(2,1)S(1)}, u32[]{:S(2)}, u32[]{:S(2)}) async-start(bf16[2,256,128]{2,0,1:T(2,128)(2,1)} %copy.64), calls=%async_computation.6 | async-start | bytes 262144 | tf_op jit(solution)/shard_map/all_to_all | solution.py:178
  228.3 0.7 copy.67
  229.1 3.8 %all-to-all-done.5 = bf16[2,256,128]{2,0,1:T(2,128)(2,1)S(1)} async-done(((bf16[2,256,128]{2,0,1:T(2,128)(2,1)}), bf16[2,256,128]{2,0,1:T(2,128)(2,1)S(1)}, u32[]{:S(2)}, u32[]{:S(2)}) %all-to-all-start.5) | async-done | bytes 131104 | tf_op jit(solution)/shard_map/all_to_all | solution.py:178
  232.9 0.7 copy.65
  (46 shorter events, 2.0 us)
Async XLA Ops:
  7.2 7.9 %all-to-all-start = ((bf16[8,64,128]{2,1,0:T(8,128)(2,1)}), bf16[8,64,128]{2,1,0:T(8,128)(2,1)S(1)}, u32[]{:S(2)}, u32[]{:S(2)}) async-start(bf16[8,64,128]{2,1,0:T(8,128)(2,1)} %param.11), calls=%async_computation | async-start | bytes 262144 | tf_op jit(solution)/shard_map/all_to_all | solution.py:25
  15.1 7.9 %all-to-all-start.1 = ((bf16[8,64,128]{2,1,0:T(8,128)(2,1)}), bf16[8,64,128]{2,1,0:T(8,128)(2,1)S(1)}, u32[]{:S(2)}, u32[]{:S(2)}) async-start(bf16[8,64,128]{2,1,0:T(8,128)(2,1)} %param.12), calls=%async_computation.1 | async-start | bytes 262144 | tf_op jit(solution)/shard_map/all_to_all | solution.py:26
  23.0 18.0 %all-to-all-start.2 = ((bf16[8,64,8,128]{3,2,1,0:T(8,128)(2,1)}), bf16[8,64,8,128]{3,2,1,0:T(8,128)(2,1)S(1)}, u32[]{:S(2)}, u32[]{:S(2)}) async-start(bf16[8,64,8,128]{3,2,1,0:T(8,128)(2,1)} %param.13), calls=%async_computation.2 | async-start | bytes 2097152 | tf_op jit(solution)/shard_map/all_to_all | solution.py:27
  41.0 80.1 %all-to-all-start.4 = ((bf16[8,64,8,128]{3,2,1,0:T(8,128)(2,1)}), bf16[8,64,8,128]{3,2,1,0:T(8,128)(2,1)}, u32[]{:S(2)}, u32[]{:S(2)}) async-start(bf16[8,64,8,128]{3,2,1,0:T(8,128)(2,1)} %param.14), calls=%async_computation.4 | async-start | bytes 2097152 | tf_op jit(solution)/shard_map/all_to_all | solution.py:28
  45.3 162.7 %reduce-scatter.2.cloned.1.call-start = ((), (), s32[]{:S(2)}) async-start(), calls=%async_computation.8 | async-start | bytes 589824 | tf_op jit(solution)/shard_map/reduce_scatter | solution.py:157
  45.5 5.5 %collective-permute-start = (f32[1,2,256]{2,0,1:T(1,128)S(1)}, f32[1,2,256]{2,0,1:T(1,128)S(1)}, u32[]{:S(2)}, u32[]{:S(2)}) collective-permute-start(f32[1,2,256]{2,0,1:T(1,128)S(1)} %slice.50), channel_id=1, source_target_pairs={{4,0},{8,4},{12,8},{16,12},{20,16},{24,20},{28,24},{5,1},{9,5},{13... | collective-permute-start | bytes 6152 | tf_op jit(solution)/shard_map/ppermute | solution.py:14
  111.0 6.5 %copy-start.4 = (bf16[512,2,256]{2,0,1:T(8,128)(2,1)}, bf16[512,2,256]{2,0,1:T(8,128)(2,1)S(1)}, u32[]{:S(2)}) copy-start(bf16[512,2,256]{2,0,1:T(8,128)(2,1)S(1)} %all_gather.7) | copy-start | bytes 1572868
  111.0 6.4 %copy-start = (bf16[2,4,64,8,128]{4,3,2,1,0:T(8,128)(2,1)}, bf16[2,4,64,8,128]{4,3,2,1,0:T(8,128)(2,1)S(1)}, u32[]{:S(2)}) copy-start(bf16[2,4,64,8,128]{4,3,2,1,0:T(8,128)(2,1)S(1)} %copy.57) | copy-start | bytes 3145732
  122.1 8.2 %copy-start.5 = (s32[2,512]{1,0:T(2,128)S(1)}, s32[2,512]{1,0:T(2,128)}, u32[]{:S(2)}) copy-start(s32[2,512]{1,0:T(2,128)} %le.55) | copy-start | bytes 12292 | tf_op jit(solution)/shard_map/cond
  123.4 1.0 copy-start.2
  124.4 5.9 %copy-start.1 = (bf16[2,2048,128]{2,1,0:T(8,128)(2,1)S(1)}, bf16[2,2048,128]{2,1,0:T(8,128)(2,1)}, u32[]{:S(2)}) copy-start(bf16[2,2048,128]{2,1,0:T(8,128)(2,1)} %get-tuple-element.117) | copy-start | bytes 3145732 | tf_op jit(solution)/shard_map/cond
  124.4 5.9 %copy-start.3 = (bf16[2,4,64,8,128]{4,3,2,1,0:T(8,128)(2,1)S(1)}, bf16[2,4,64,8,128]{4,3,2,1,0:T(8,128)(2,1)}, u32[]{:S(2)}) copy-start(bf16[2,4,64,8,128]{4,3,2,1,0:T(8,128)(2,1)} %copy-done.2) | copy-start | bytes 3145732 | tf_op jit(solution)/shard_map/cond
  145.1 71.9 %all-to-all-start.3 = ((bf16[2,256,8,128]{3,2,0,1:T(8,128)(2,1)}), bf16[2,256,8,128]{3,2,0,1:T(8,128)(2,1)S(1)}, u32[]{:S(2)}, u32[]{:S(2)}) async-start(bf16[2,256,8,128]{3,2,0,1:T(8,128)(2,1)} %copy.58), calls=%async_computation.3 | async-start | bytes 2097152 | tf_op jit(solution)/shard_map/all_to_all | solution.py:124
  208.6 6.4 %collective-permute-start.1 = (bf16[1,2,256]{2,0,1:T(2,128)(2,1)S(1)}, bf16[1,2,256]{2,0,1:T(2,128)(2,1)S(1)}, u32[]{:S(2)}, u32[]{:S(2)}) collective-permute-start(bf16[1,2,256]{2,0,1:T(2,128)(2,1)S(1)} %slice.52), channel_id=1, source_target_pairs={{0,4},{4,8},{8,12},{12,16},{16,20},{20,24},{24,28},{1,5},{5,9},{9,... | collective-permute-start | bytes 3080 | tf_op jit(solution)/shard_map/ppermute | solution.py:14
  217.0 7.9 %all-to-all-start.6 = ((bf16[2,256,128]{2,0,1:T(2,128)(2,1)}), bf16[2,256,128]{2,0,1:T(2,128)(2,1)S(1)}, u32[]{:S(2)}, u32[]{:S(2)}) async-start(bf16[2,256,128]{2,0,1:T(2,128)(2,1)} %copy.66), calls=%async_computation.7 | async-start | bytes 262144 | tf_op jit(solution)/shard_map/all_to_all | solution.py:185
  224.9 7.9 %all-to-all-start.5 = ((bf16[2,256,128]{2,0,1:T(2,128)(2,1)}), bf16[2,256,128]{2,0,1:T(2,128)(2,1)S(1)}, u32[]{:S(2)}, u32[]{:S(2)}) async-start(bf16[2,256,128]{2,0,1:T(2,128)(2,1)} %copy.64), calls=%async_computation.6 | async-start | bytes 262144 | tf_op jit(solution)/shard_map/all_to_all | solution.py:178
Sparse Core Ops, SparseCore 0:
  144.1 63.8 reduce-scatter.1
where the time goes:
time: 242 us; the launch traced here: 241 us
  waiting for transfers between devices  90.6 us (37%)
  blocking collectives  59.9 us (25%)
  starting transfers between devices  31.3 us (13%)
  matrix products  24.4 us (10%)
  between operations  14.9 us (6%)
  local copies, waits for them, and re-layouts  11 us (5%)
  other arithmetic  8.1 us (3%)
    reduce_scatter x1, waiting for transfers between devices, per_device(): lax.psum_scatter(partials.astype(jnp.bfloat16), 'ctx', scatter_dimension=...  59.2 us
    all_gather x1, blocking collectives, per_device(): pair_block = lax.all_gather(slot_pairs, 'ctx', axis=0, tiled=True)  31.5 us
    all_gather x1, blocking collectives, per_device(): lax.all_gather(slot_pairs[:, :, :head_dim], 'ctx', axis=0, tiled=True)  28.4 us
    all_to_all x1, waiting for transfers between devices, per_device(): lax.all_to_all(queries, 'head', split_axis=0, concat_axis=1, tiled=True)  13.4 us
    dot_general x2, matrix products, block_scores(): jnp.einsum('hrd,nhd->hrn', query_rows, key_block, preferred_element_type=...  7.21 us
    dot_general x1, matrix products, grad_advance(): jnp.einsum('hrn,hrd->nhd', dscores, query_rows, preferred_element_type=jn...  6.96 us
    ppermute x2, starting transfers between devices, from_behind(): lax.ppermute(value, axis, [(source, source + steps) for source in range(i...  6.64 us
    dot_general x1, matrix products, grad_advance(): jnp.einsum('hrn,hrd->nhd', weights_low, grad_rows, preferred_element_type...  5.63 us
  transfers between devices with their start and end apart: 10, of which 8 were waited for; matrix products, arithmetic and copies ran while one was open for 8% of the time, Pallas kernels for 0%

commit v1 on v0

--- a/solution.py
+++ b/solution.py
@@ -3,9 +3,31 @@
 import jax.numpy as jnp
 from jax import lax
 from jax.sharding import PartitionSpec as P
+from jax.lax import axis_index, axis_size, ppermute
 
 RATIO = 4
 neg_big = -1e30
+
+
+def manage_the_field(mine_x, named_axis):
+    formed, small = (axis_size(named_axis), axis_index(named_axis))
+    r2 = list(mine_x.shape)
+    r_now = mine_x.shape[0] // formed
+    r2[0] = r_now
+    current_value = r2[1]
+    r2[1] = current_value * formed
+    block_next = jnp.zeros(r2, mine_x.dtype)
+    for ii in [*range(formed)]:
+        val2 = lax.dynamic_slice_in_dim(mine_x, (small ^ ii) * r_now, r_now, axis=0)
+        if ii:
+            kept_rows = []
+            for dev_i in [*range(formed)]:
+                kept_rows.append((dev_i, dev_i ^ ii))
+            val2 = ppermute(val2, named_axis, kept_rows)
+        block_next = lax.dynamic_update_slice_in_dim(
+            block_next, val2, (small ^ ii) * current_value, axis=1
+        )
+    return block_next
 
 
 def from_behind(value, axis, steps):
@@ -23,7 +45,7 @@
 def per_device(token_keys, token_values, queries, out_grad, slot_ids):
     keys_here, values_here, query_here, grad_here = (
         lax.all_to_all(token_keys, "head", split_axis=0, concat_axis=1, tiled=True),
-        lax.all_to_all(token_values, "head", split_axis=0, concat_axis=1, tiled=True),
+        manage_the_field(token_values, "head"),
         lax.all_to_all(queries, "head", split_axis=0, concat_axis=1, tiled=True),
         lax.all_to_all(out_grad, "head", split_axis=0, concat_axis=1, tiled=True),
     )

time: 242 us -> 235 us (0.971)
  waiting for transfers between devices: 90.6 us -> 83.6 us
    all_to_all x1 -> x0, waiting for transfers between devices: 4.58 us -> none  [per_device(): lax.all_to_all(token_values, 'head', split_axis=0, concat_axis=1, tiled=T...]
    all_to_all x1 -> x0, starting transfers between devices: 3.33 us -> none  [per_device(): lax.all_to_all(token_values, 'head', split_axis=0, concat_axis=1, tiled=T...]
    all_to_all x1, waiting for transfers between devices: 2.63 us -> 0.01 us  [per_device(): lax.all_to_all(token_keys, 'head', split_axis=0, concat_axis=1, tiled=True)]
  transfers between devices with their start and end apart: 10 -> 12, of which waited for: 8 -> 6; matrix products, arithmetic and copies ran while one was open for 8% -> 9% of each run, Pallas kernels for 0% -> 0%
where the time goes in v1:
time: 235 us; the launch traced here: 233 us
  waiting for transfers between devices  83.6 us (36%)
  blocking collectives  59.9 us (25%)
  starting transfers between devices  30.3 us (13%)
  matrix products  24.5 us (10%)
  between operations  14.9 us (6%)
  local copies, waits for them, and re-layouts  11.9 us (5%)
  other arithmetic  8.11 us (3%)
    reduce_scatter x1, waiting for transfers between devices, per_device(): lax.psum_scatter(partials.astype(jnp.bfloat16), 'ctx', scatter_dimension=...  59.2 us
    all_gather x1, blocking collectives, per_device(): pair_block = lax.all_gather(slot_pairs, 'ctx', axis=0, tiled=True)  31.5 us
    all_gather x1, blocking collectives, per_device(): lax.all_gather(slot_pairs[:, :, :head_dim], 'ctx', axis=0, tiled=True)  28.4 us
    all_to_all x1, waiting for transfers between devices, per_device(): lax.all_to_all(queries, 'head', split_axis=0, concat_axis=1, tiled=True)  13.6 us
    dot_general x2, matrix products, block_scores(): jnp.einsum('hrd,nhd->hrn', query_rows, key_block, preferred_element_type=...  7.24 us
    dot_general x1, matrix products, grad_advance(): jnp.einsum('hrn,hrd->nhd', dscores, query_rows, preferred_element_type=jn...  6.96 us
    ppermute x2, starting transfers between devices, from_behind(): lax.ppermute(value, axis, [(source, source + steps) for source in range(i...  6.65 us
    dot_general x1, matrix products, grad_advance(): jnp.einsum('hrn,hrd->nhd', weights_low, grad_rows, preferred_element_type...  5.63 us
  transfers between devices with their start and end apart: 12, of which 6 were waited for; matrix products, arithmetic and copies ran while one was open for 9% of the time, Pallas kernels for 0%

profile of v1, /device:TPU:8, one launch (start us, length us, event | category | flops | bytes accessed | tf_op | source)
XLA Modules:
  0.0 233.4 jit_solution(11360850656277990461)
XLA Ops:
  7.2 3.3 %all-to-all-start = ((bf16[8,64,128]{2,1,0:T(8,128)(2,1)}), bf16[8,64,128]{2,1,0:T(8,128)(2,1)S(1)}, u32[]{:S(2)}, u32[]{:S(2)}) async-start(bf16[8,64,128]{2,1,0:T(8,128)(2,1)} %param.11), calls=%async_computation | async-start | bytes 262144 | tf_op jit(solution)/shard_map/all_to_all | solution.py:47
  10.6 0.8 constant_dynamic-slice_fusion.2
  11.4 1.8 collective-permute-start.2
  13.2 0.4 collective-permute-start
  13.9 0.7 copy.68
  14.6 0.5 convert_reduce_fusion
  15.3 0.6 slice_reduce_fusion
  15.9 3.5 %all-to-all-start.1 = ((bf16[8,64,8,128]{3,2,1,0:T(8,128)(2,1)}), bf16[8,64,8,128]{3,2,1,0:T(8,128)(2,1)S(1)}, u32[]{:S(2)}, u32[]{:S(2)}) async-start(bf16[8,64,8,128]{3,2,1,0:T(8,128)(2,1)} %param.13), calls=%async_computation.1 | async-start | bytes 2097152 | tf_op jit(solution)/shard_map/all_to_all | solution.py:49
  19.4 0.7 fusion.38
  20.3 13.6 %all-to-all-done.1 = bf16[8,64,8,128]{3,2,1,0:T(8,128)(2,1)S(1)} async-done(((bf16[8,64,8,128]{3,2,1,0:T(8,128)(2,1)}), bf16[8,64,8,128]{3,2,1,0:T(8,128)(2,1)S(1)}, u32[]{:S(2)}, u32[]{:S(2)}) %all-to-all-start.1) | async-done | bytes 1048608 | tf_op jit(solution)/shard_map/all_to_all | solution.py:49
  33.9 4.3 %all-to-all-start.3 = ((bf16[8,64,8,128]{3,2,1,0:T(8,128)(2,1)}), bf16[8,64,8,128]{3,2,1,0:T(8,128)(2,1)}, u32[]{:S(2)}, u32[]{:S(2)}) async-start(bf16[8,64,8,128]{3,2,1,0:T(8,128)(2,1)} %param.14), calls=%async_computation.3 | async-start | bytes 2097152 | tf_op jit(solution)/shard_map/all_to_all | solution.py:50
  38.2 0.2 convolution_bitcast_fusion
  38.4 3.3 %collective-permute-start.3 = (f32[1,2,256]{2,0,1:T(1,128)S(1)}, f32[1,2,256]{2,0,1:T(1,128)S(1)}, u32[]{:S(2)}, u32[]{:S(2)}) collective-permute-start(f32[1,2,256]{2,0,1:T(1,128)S(1)} %slice.50), channel_id=1, source_target_pairs={{4,0},{8,4},{12,8},{16,12},{20,16},{24,20},{28,24},{5,1},{9,5},{13... | collective-permute-start | bytes 6152 | tf_op jit(solution)/shard_map/ppermute | solution.py:36
  42.4 1.5 collective-permute-done.3
  44.0 28.4 %all_gather.8 = bf16[512,2,128]{2,0,1:T(8,128)(2,1)S(1)} all-gather(bf16[64,2,128]{2,0,1:T(8,128)(2,1)S(1)} %slice.51), channel_id=1, replica_groups=mesh['ctx'=8,'head'=4] {'ctx'}, dimensions={0}, use_global_device_ids=true | all-gather | bytes 294912 | tf_op jit(solution)/shard_map/all_gather | solution.py:114
  72.3 31.5 %all_gather.7 = bf16[512,2,256]{2,0,1:T(8,128)(2,1)S(1)} all-gather(bf16[64,2,256]{2,0,1:T(8,128)(2,1)S(1)} %fusion.31), channel_id=1, replica_groups=mesh['ctx'=8,'head'=4] {'ctx'}, dimensions={0}, use_global_device_ids=true | all-gather | bytes 589824 | tf_op jit(solution)/shard_map/all_gather | solution.py:133
  104.0 5.0 %conditional.3 = (f32[2,2048]{1,0:T(2,128)}, f32[2,2048]{1,0:T(2,128)S(1)}) conditional(s32[]{:T(128)} %convert_element_type.72, () %tuple.34, (s32[2,8,64]{2,1,0:T(8,128)S(1)}, s32[256,8]{1,0:T(8,128)S(1)}, bf16[2,2048,128]{2,1,0:T(8,128)(2,1)S(1)}, bf16[512,2,128]{2,0,1:T(8,128)(2,1)S(1)}) %tuple.59), branch_computations={%region_2.3_spmd, %region_3.6_spmd} | conditional | flops 555741184 | bytes 18251792 | solution.py:123
  104.2 1.3 fusion
  105.6 0.6 broadcast_maximum_fusion
  106.2 2.7 %fusion.1 = f32[2,2048]{1,0:T(2,128)S(1)} fusion(f32[2,2048,512]{1,2,0:T(8,128)S(1)} %get-tuple-element.122, f32[2,2048]{1,0:T(2,128)} %broadcast_maximum_fusion, s32[2048]{0:T(1024)S(1)} %le.37, s32[2,512]{1,0:T(2,128)S(1)} %le.35), kind=kLoop, calls=%fused_computation.3 | loop fusion | flops 10481664 | bytes 8433664 | tf_op jit(solution)/shard_map/cond/branch_1_fun/reduce_sum | solution.py:120
  109.0 1.3 add.130
  110.3 3.5 %conditional.4 = (bf16[2,2048,128]{2,1,0:T(8,128)(2,1)S(1)}) conditional(s32[]{:T(128)} %convert_element_type.72, () %tuple.33, (s32[2,8,64]{2,1,0:T(8,128)S(1)}, s32[256,8]{1,0:T(8,128)S(1)}, bf16[512,2,256]{2,0,1:T(8,128)(2,1)S(1)}, bf16[2,2048,128]{2,1,0:T(8,128)(2,1)S(1)}, f32[2,2048]{1,0:T(2,128)}) %tuple.60), branch_computations={%region_6.7_spmd, %region_7.8_spmd} | conditional | flops 1084227584 | bytes 2674696 | solution.py:144
  110.5 3.3 %fusion.2 = bf16[2,2048,128]{2,1,0:T(8,128)(2,1)S(1)} fusion(bf16[2,2048,128]{2,1,0:T(8,128)(2,1)S(1)} %get-tuple-element.67, f32[2,2048]{1,0:T(2,128)} %get-tuple-element.69, s32[2,512]{1,0:T(2,128)S(1)} %le.50, s32[2048]{0:T(1024)S(1)} %le.52, bf16[512,2,256]{2,0,1:T(8,128)(2,1)S(1)} %get-tuple-element.68), kind=kOutput, calls=%fused_computation.6 | convolution fusion | flops 1084227584 | bytes 2650112 | tf_op jit(solution)/shard_map/cond/branch_1_fun/hrn,nhd->hrd/dot_general | solution.py:137
  114.0 21.8 %conditional.5 = (bf16[512,2,256]{0,2,1:T(8,128)(2,1)S(1)}) conditional(s32[]{:T(128)} %convert_element_type.72, () %tuple.37, (s32[2,8,64]{2,1,0:T(8,128)S(1)}, s32[256,8]{1,0:T(8,128)S(1)}, bf16[512,2,256]{2,0,1:T(8,128)(2,1)}, bf16[2,2048,128]{2,1,0:T(8,128)(2,1)}, f32[2,2048]{1,0:T(2,128)}, /*index=5*/bf16[2,4,64,8,128]{4,3,2,0,1:T(8,128)(2,1)}, ...), branch_computations={%region_8.9_spmd, %region_9.11_spmd} | conditional | flops 2175528960 | bytes 49414264 | solution.py:176
  114.2 0.7 le.55
  115.0 1.3 copy.57
  116.3 0.7 multiply_reduce_fusion
  117.0 0.3 copy-done.2
  117.2 5.9 %fusion.20 = f32[2,2048,512]{2,1,0:T(8,128)} fusion(bf16[2,2048,128]{2,1,0:T(8,128)(2,1)} %get-tuple-element.117, bf16[512,2,256]{2,0,1:T(8,128)(2,1)} %get-tuple-element.73), kind=kOutput, calls=%fused_computation.23 | convolution fusion | flops 536870912 | bytes 9699328 | tf_op jit(solution)/shard_map/cond/branch_1_fun/hrd,nhd->hrn/dot_general | solution.py:98
  123.1 7.0 %fusion.17 = bf16[512,2,128]{0,2,1:T(8,128)(2,1)S(1)} fusion(bf16[2,2048,128]{2,1,0:T(8,128)(2,1)S(1)} %copy-done.1, f32[2,2048,512]{2,1,0:T(8,128)} %fusion.20, bf16[2,2048,128]{2,1,0:T(8,128)(2,1)S(1)} %bitcast.53, f32[2,2048]{1,0:T(2,128)S(1)} %multiply_reduce_fusion, f32[2,2048]{1,0:T(2,128)} %get-tuple-element.74, s32[2,512]{1,0:T(2,128)S(1)} %copy-done.5, ...), kind=kOutput, calls=%fused_computation.20 | convolution fusion | flops 1088684032 | bytes 11055104 | tf_op jit(solution)/shard_map/cond/branch_1_fun/hrn,hrd->nhd/dot_general | solution.py:171
  130.1 5.6 %fusion.13 = bf16[512,2,128]{0,2,1:T(8,128)(2,1)S(1)} fusion(bf16[2,2048,128]{2,1,0:T(8,128)(2,1)S(1)} %bitcast.54, f32[2,2048,512]{2,1,0:T(8,128)} %fusion.20, f32[2,2048]{1,0:T(2,128)} %get-tuple-element.74, s32[2,512]{1,0:T(2,128)S(1)} %copy-done.5, s32[2048]{0:T(1024)S(1)} %le.57), kind=kOutput, calls=%fused_computation.18 | convolution fusion | flops 547356672 | bytes 9728000 | tf_op jit(solution)/shard_map/cond/branch_1_fun/hrn,hrd->nhd/dot_general | solution.py:160
  135.8 1.0 copy.58
  136.8 1.2 copy.53
  138.0 3.5 %all-to-all-start.2 = ((bf16[2,256,8,128]{3,2,0,1:T(8,128)(2,1)}), bf16[2,256,8,128]{3,2,0,1:T(8,128)(2,1)S(1)}, u32[]{:S(2)}, u32[]{:S(2)}) async-start(bf16[2,256,8,128]{3,2,0,1:T(8,128)(2,1)} %copy.53), calls=%async_computation.2 | async-start | bytes 2097152 | tf_op jit(solution)/shard_map/all_to_all | solution.py:146
  141.6 59.2 %reduce-scatter.2.cloned.1.call-done = bf16[64,2,256]{2,0,1:T(8,128)(2,1)} async-done(((bf16[512,2,256]{2,0,1:T(8,128)(2,1)}), bf16[64,2,256]{2,0,1:T(8,128)(2,1)}) %reduce-scatter.2.cloned.1.call-update) | async-done | bytes 65552 | tf_op jit(solution)/shard_map/reduce_scatter | solution.py:179
  200.8 0.7 slice.52
  201.5 3.4 %collective-permute-start.4 = (bf16[1,2,256]{2,0,1:T(2,128)(2,1)S(1)}, bf16[1,2,256]{2,0,1:T(2,128)(2,1)S(1)}, u32[]{:S(2)}, u32[]{:S(2)}) collective-permute-start(bf16[1,2,256]{2,0,1:T(2,128)(2,1)S(1)} %slice.52), channel_id=1, source_target_pairs={{0,4},{4,8},{8,12},{12,16},{16,20},{20,24},{24,28},{1,5},{5,9},{9,... | collective-permute-start | bytes 3080 | tf_op jit(solution)/shard_map/ppermute | solution.py:36
  205.0 2.9 %collective-permute-done.4 = bf16[1,2,256]{2,0,1:T(2,128)(2,1)S(1)} collective-permute-done((bf16[1,2,256]{2,0,1:T(2,128)(2,1)S(1)}, bf16[1,2,256]{2,0,1:T(2,128)(2,1)S(1)}, u32[]{:S(2)}, u32[]{:S(2)}) %collective-permute-start.4) | collective-permute-done | bytes 1056 | tf_op jit(solution)/shard_map/ppermute | solution.py:36
  207.8 1.1 fusion.26
  209.0 0.8 copy.61
  209.8 3.3 %all-to-all-start.5 = ((bf16[2,256,128]{2,0,1:T(2,128)(2,1)}), bf16[2,256,128]{2,0,1:T(2,128)(2,1)S(1)}, u32[]{:S(2)}, u32[]{:S(2)}) async-start(bf16[2,256,128]{2,0,1:T(2,128)(2,1)} %copy.61), calls=%async_computation.6 | async-start | bytes 262144 | tf_op jit(solution)/shard_map/all_to_all | solution.py:207
  213.2 1.2 copy.55
  214.3 0.8 copy.59
  215.1 2.6 %all-to-all-done.5 = bf16[2,256,128]{2,0,1:T(2,128)(2,1)S(1)} async-done(((bf16[2,256,128]{2,0,1:T(2,128)(2,1)}), bf16[2,256,128]{2,0,1:T(2,128)(2,1)S(1)}, u32[]{:S(2)}, u32[]{:S(2)}) %all-to-all-start.5) | async-done | bytes 131104 | tf_op jit(solution)/shard_map/all_to_all | solution.py:207
  217.8 3.3 %all-to-all-start.4 = ((bf16[2,256,128]{2,0,1:T(2,128)(2,1)}), bf16[2,256,128]{2,0,1:T(2,128)(2,1)S(1)}, u32[]{:S(2)}, u32[]{:S(2)}) async-start(bf16[2,256,128]{2,0,1:T(2,128)(2,1)} %copy.59), calls=%async_computation.5 | async-start | bytes 262144 | tf_op jit(solution)/shard_map/all_to_all | solution.py:200
  221.2 0.7 copy.62
  221.9 3.8 %all-to-all-done.4 = bf16[2,256,128]{2,0,1:T(2,128)(2,1)S(1)} async-done(((bf16[2,256,128]{2,0,1:T(2,128)(2,1)}), bf16[2,256,128]{2,0,1:T(2,128)(2,1)S(1)}, u32[]{:S(2)}, u32[]{:S(2)}) %all-to-all-start.4) | async-done | bytes 131104 | tf_op jit(solution)/shard_map/all_to_all | solution.py:200
  225.8 0.7 copy.60
  (54 shorter events, 2.2 us)
Async XLA Ops:
  7.2 8.7 %all-to-all-start = ((bf16[8,64,128]{2,1,0:T(8,128)(2,1)}), bf16[8,64,128]{2,1,0:T(8,128)(2,1)S(1)}, u32[]{:S(2)}, u32[]{:S(2)}) async-start(bf16[8,64,128]{2,1,0:T(8,128)(2,1)} %param.11), calls=%async_computation | async-start | bytes 262144 | tf_op jit(solution)/shard_map/all_to_all | solution.py:47
  11.4 8.8 %collective-permute-start.2 = (bf16[2,64,128]{2,1,0:T(8,128)(2,1)S(1)}, bf16[2,64,128]{2,1,0:T(8,128)(2,1)S(1)}, u32[]{:S(2)}, u32[]{:S(2)}) collective-permute-start(bf16[2,64,128]{2,1,0:T(8,128)(2,1)S(1)} %get-tuple-element.125), channel_id=1, source_target_pairs={{0,3},{1,2},{2,1},{3,0},{4,7},{5,6},{6,5},{7,4},{8,11},{9,10},{10,... | collective-permute-start | bytes 98312 | tf_op jit(solution)/shard_map/ppermute | solution.py:26
  13.2 7.0 %collective-permute-start = (bf16[2,64,128]{2,1,0:T(8,128)(2,1)S(1)}, bf16[2,64,128]{2,1,0:T(8,128)(2,1)S(1)}, u32[]{:S(2)}, u32[]{:S(2)}) collective-permute-start(bf16[2,64,128]{2,1,0:T(8,128)(2,1)S(1)} %get-tuple-element.126), channel_id=1, source_target_pairs={{0,1},{1,0},{2,3},{3,2},{4,5},{5,4},{6,7},{7,6},{8,9},{9,8},{10,11... | collective-permute-start | bytes 98312 | tf_op jit(solution)/shard_map/ppermute | solution.py:26
  13.5 6.7 %collective-permute-start.1 = (bf16[2,64,128]{2,1,0:T(8,128)(2,1)S(1)}, bf16[2,64,128]{2,1,0:T(8,128)(2,1)S(1)}, u32[]{:S(2)}, u32[]{:S(2)}) collective-permute-start(bf16[2,64,128]{2,1,0:T(8,128)(2,1)S(1)} %get-tuple-element.128), channel_id=1, source_target_pairs={{0,2},{1,3},{2,0},{3,1},{4,6},{5,7},{6,4},{7,5},{8,10},{9,11},{10,... | collective-permute-start | bytes 98312 | tf_op jit(solution)/shard_map/ppermute | solution.py:26
  15.9 18.0 %all-to-all-start.1 = ((bf16[8,64,8,128]{3,2,1,0:T(8,128)(2,1)}), bf16[8,64,8,128]{3,2,1,0:T(8,128)(2,1)S(1)}, u32[]{:S(2)}, u32[]{:S(2)}) async-start(bf16[8,64,8,128]{3,2,1,0:T(8,128)(2,1)} %param.13), calls=%async_computation.1 | async-start | bytes 2097152 | tf_op jit(solution)/shard_map/all_to_all | solution.py:49
  33.9 80.1 %all-to-all-start.3 = ((bf16[8,64,8,128]{3,2,1,0:T(8,128)(2,1)}), bf16[8,64,8,128]{3,2,1,0:T(8,128)(2,1)}, u32[]{:S(2)}, u32[]{:S(2)}) async-start(bf16[8,64,8,128]{3,2,1,0:T(8,128)(2,1)} %param.14), calls=%async_computation.3 | async-start | bytes 2097152 | tf_op jit(solution)/shard_map/all_to_all | solution.py:50
  38.1 162.6 %reduce-scatter.2.cloned.1.call-start = ((), (), s32[]{:S(2)}) async-start(), calls=%async_computation.7 | async-start | bytes 589824 | tf_op jit(solution)/shard_map/reduce_scatter | solution.py:179
  38.4 5.5 %collective-permute-start.3 = (f32[1,2,256]{2,0,1:T(1,128)S(1)}, f32[1,2,256]{2,0,1:T(1,128)S(1)}, u32[]{:S(2)}, u32[]{:S(2)}) collective-permute-start(f32[1,2,256]{2,0,1:T(1,128)S(1)} %slice.50), channel_id=1, source_target_pairs={{4,0},{8,4},{12,8},{16,12},{20,16},{24,20},{28,24},{5,1},{9,5},{13... | collective-permute-start | bytes 6152 | tf_op jit(solution)/shard_map/ppermute | solution.py:36
  103.8 6.5 %copy-start.4 = (bf16[512,2,256]{2,0,1:T(8,128)(2,1)}, bf16[512,2,256]{2,0,1:T(8,128)(2,1)S(1)}, u32[]{:S(2)}) copy-start(bf16[512,2,256]{2,0,1:T(8,128)(2,1)S(1)} %all_gather.7) | copy-start | bytes 1572868
  103.9 6.4 %copy-start = (bf16[2,4,64,8,128]{4,3,2,1,0:T(8,128)(2,1)}, bf16[2,4,64,8,128]{4,3,2,1,0:T(8,128)(2,1)S(1)}, u32[]{:S(2)}) copy-start(bf16[2,4,64,8,128]{4,3,2,1,0:T(8,128)(2,1)S(1)} %copy.52) | copy-start | bytes 3145732
  115.0 8.2 %copy-start.5 = (s32[2,512]{1,0:T(2,128)S(1)}, s32[2,512]{1,0:T(2,128)}, u32[]{:S(2)}) copy-start(s32[2,512]{1,0:T(2,128)} %le.55) | copy-start | bytes 12292 | tf_op jit(solution)/shard_map/cond
  116.3 1.0 copy-start.2
  117.2 5.9 %copy-start.1 = (bf16[2,2048,128]{2,1,0:T(8,128)(2,1)S(1)}, bf16[2,2048,128]{2,1,0:T(8,128)(2,1)}, u32[]{:S(2)}) copy-start(bf16[2,2048,128]{2,1,0:T(8,128)(2,1)} %get-tuple-element.117) | copy-start | bytes 3145732 | tf_op jit(solution)/shard_map/cond
  117.2 5.9 %copy-start.3 = (bf16[2,4,64,8,128]{4,3,2,1,0:T(8,128)(2,1)S(1)}, bf16[2,4,64,8,128]{4,3,2,1,0:T(8,128)(2,1)}, u32[]{:S(2)}) copy-start(bf16[2,4,64,8,128]{4,3,2,1,0:T(8,128)(2,1)} %copy-done.2) | copy-start | bytes 3145732 | tf_op jit(solution)/shard_map/cond
  138.0 71.8 %all-to-all-start.2 = ((bf16[2,256,8,128]{3,2,0,1:T(8,128)(2,1)}), bf16[2,256,8,128]{3,2,0,1:T(8,128)(2,1)S(1)}, u32[]{:S(2)}, u32[]{:S(2)}) async-start(bf16[2,256,8,128]{3,2,0,1:T(8,128)(2,1)} %copy.53), calls=%async_computation.2 | async-start | bytes 2097152 | tf_op jit(solution)/shard_map/all_to_all | solution.py:146
  201.5 6.4 %collective-permute-start.4 = (bf16[1,2,256]{2,0,1:T(2,128)(2,1)S(1)}, bf16[1,2,256]{2,0,1:T(2,128)(2,1)S(1)}, u32[]{:S(2)}, u32[]{:S(2)}) collective-permute-start(bf16[1,2,256]{2,0,1:T(2,128)(2,1)S(1)} %slice.52), channel_id=1, source_target_pairs={{0,4},{4,8},{8,12},{12,16},{16,20},{20,24},{24,28},{1,5},{5,9},{9,... | collective-permute-start | bytes 3080 | tf_op jit(solution)/shard_map/ppermute | solution.py:36
  209.8 7.9 %all-to-all-start.5 = ((bf16[2,256,128]{2,0,1:T(2,128)(2,1)}), bf16[2,256,128]{2,0,1:T(2,128)(2,1)S(1)}, u32[]{:S(2)}, u32[]{:S(2)}) async-start(bf16[2,256,128]{2,0,1:T(2,128)(2,1)} %copy.61), calls=%async_computation.6 | async-start | bytes 262144 | tf_op jit(solution)/shard_map/all_to_all | solution.py:207
  217.8 7.9 %all-to-all-start.4 = ((bf16[2,256,128]{2,0,1:T(2,128)(2,1)}), bf16[2,256,128]{2,0,1:T(2,128)(2,1)S(1)}, u32[]{:S(2)}, u32[]{:S(2)}) async-start(bf16[2,256,128]{2,0,1:T(2,128)(2,1)} %copy.59), calls=%async_computation.5 | async-start | bytes 262144 | tf_op jit(solution)/shard_map/all_to_all | solution.py:200
Sparse Core Ops, SparseCore 0:
  136.9 63.7 reduce-scatter.1
